TPU v7x, 256 devices: a whole 4x4x8 slice. The times are simulated.
256 devices in a mesh: pipe: 8 (over z), seq: 16 (over x, y), tp: 2 (over core).
Axes of the slice: x: 4, y: 4, z: 8, core: 2. Of those that a mesh axis runs over, the one named last changes fastest.
Arguments:
- layer_inputs: bfloat16 [8, 2048, 4096], P('pipe', ('seq', 'tp')), may hold values from -6 to 6
- out_grad: bfloat16 [2048, 4096], P('seq', 'tp'), may hold values from -6 to 6
- short_weights: bfloat16 [8, 7, 3, 4096], P('pipe', None, None, 'tp'), may hold values from -2 to 2
- long_filters: bfloat16 [8, 256, 128], P('pipe', 'tp'), may hold values from -0.15625 to 0.15625
- out_weights: bfloat16 [8, 4096, 4096], P('pipe', 'tp', 'seq'), may hold values from -0.09375 to 0.09375
Outputs:
- input_grad: bfloat16 [8, 2048, 4096], P('pipe', 'seq', 'tp')
- short_grad: float32 [8, 7, 3, 4096], P('pipe', None, None, 'tp')
- long_grad: float32 [8, 256, 128], P('pipe', 'tp')
All inputs are finite; a program needn't handle non-finite values.
Results may differ from a plain program's by a relative error of at most 0.03.
Values may be sent and summed in bfloat16 or wider, within the bound.
No kernel may reach another device: no remote copies, remote signals or barrier semaphores. Data moves between devices by JAX's collectives and lax.ppermute only.
A program may use at most 192 MiB of HBM per device.

v0:
```python
import jax
import jax.numpy as jnp
from jax import lax
from jax.sharding import PartitionSpec as P


def passed_along(array, axis, by):
    size = lax.axis_size(axis)
    pairs = [(i, i + by) for i in range(size) if 0 <= i + by < size]
    return lax.ppermute(array, axis, pairs)


def toeplitz_blocks(filters):
    groups, kernel_width = filters.shape
    base_row = jnp.concatenate(
        [
            jnp.zeros((groups, 1), filters.dtype),
            filters[:, ::-1],
            jnp.zeros((groups, kernel_width), filters.dtype),
        ],
        axis=1,
    )
    tiled = jnp.tile(base_row, (1, kernel_width))[:, : 2 * kernel_width * kernel_width]
    return tiled.reshape(groups, kernel_width, 2 * kernel_width)


def lag_sums(products):
    groups, kernel_width, window = products.shape
    flattened = products.reshape(groups, kernel_width * window)
    flattened = jnp.pad(flattened, ((0, 0), (0, kernel_width)))
    skewed = flattened.reshape(groups, kernel_width, window + 1)
    totals = jnp.sum(skewed, axis=1)
    return totals[:, 1 : kernel_width + 1][:, ::-1]


def to_groups(rows, groups):
    count = rows.shape[0]
    return jnp.transpose(rows.reshape(count, groups, rows.shape[1] // groups), (1, 2, 0))


def from_groups(blocks):
    groups, width, count = blocks.shape
    return jnp.transpose(blocks, (2, 0, 1)).reshape(count, groups * width)


def featurize(source, weights):
    tap_count = weights.shape[0]
    row_count = source.shape[0] - tap_count + 1
    running = jnp.zeros((weights.shape[1], row_count, source.shape[1]), jnp.float32)
    for offset in range(tap_count):
        start = tap_count - 1 - offset
        running = running + weights[offset][:, None, :] * source[start : start + row_count][None]
    return running


def spread_back(feature_grads, weights):
    tap_count = weights.shape[0]
    row_count = feature_grads.shape[1] - tap_count + 1
    running = jnp.zeros((row_count, feature_grads.shape[2]), jnp.float32)
    for offset in range(tap_count):
        running = running + jnp.sum(
            weights[offset][:, None, :] * feature_grads[:, offset : offset + row_count], axis=0
        )
    return running


def weight_grads(feature_grads, source):
    row_count = feature_grads.shape[1]
    tap_count = source.shape[0] - row_count + 1
    terms = []
    for offset in range(tap_count):
        start = tap_count - 1 - offset
        terms.append(jnp.sum(feature_grads * source[start : start + row_count][None], axis=1))
    return jnp.stack(terms)


def long_forward(padded, toeplitz, groups):
    grouped = to_groups(padded, groups)
    result = jnp.einsum("gis,gcs->gci", toeplitz, grouped, preferred_element_type=jnp.float32)
    return from_groups(result)


def long_backward(trailing, reversed_band, groups):
    grouped = to_groups(trailing, groups)
    result = jnp.einsum("grj,gcr->gcj", reversed_band, grouped, preferred_element_type=jnp.float32)
    return from_groups(result)


def filter_grads(mixed_grad, padded, groups):
    grad_groups = to_groups(mixed_grad, groups)
    value_groups = to_groups(padded, groups)
    products = jnp.einsum(
        "gci,gcs->gis", grad_groups, value_groups, preferred_element_type=jnp.float32
    )
    return lag_sums(products)


def recompute(layer_block, weights, filters):
    local_rows = lax.all_to_all(layer_block, "tp", split_axis=1, concat_axis=0, tiled=True)
    tap_count = weights.shape[0]
    kernel_width = filters.shape[1]
    before = passed_along(local_rows[local_rows.shape[0] - tap_count + 1 :], "seq", 1)
    extended = jnp.concatenate([before, local_rows], axis=0).astype(jnp.float32)
    features = featurize(extended, weights)
    products = (features[1] * features[2]).astype(jnp.bfloat16)
    earlier_products = passed_along(products[products.shape[0] - kernel_width + 1 :], "seq", 1)
    padded = jnp.concatenate(
        [jnp.zeros((1, products.shape[1]), jnp.bfloat16), earlier_products, products], axis=0
    )
    toeplitz = toeplitz_blocks(filters)
    reversed_band = jnp.concatenate(
        [toeplitz[:, :, kernel_width:], toeplitz[:, :, :kernel_width]], axis=1
    )
    mixed_rows = long_forward(padded, toeplitz, filters.shape[0])
    return (features, padded, reversed_band, mixed_rows, extended)


def dense_grad(incoming, columns, active):
    empty_sum = jnp.zeros((incoming.shape[0], columns.shape[0]), jnp.float32)
    piece = lax.all_gather(incoming, "tp", axis=1, tiled=True)
    summed = lax.cond(
        active,
        lambda: jnp.einsum("td,cd->tc", piece, columns, preferred_element_type=jnp.float32),
        lambda: empty_sum,
    )
    return summed.astype(jnp.bfloat16)


def backward(saved_state, incoming, dense_part, weights, groups, active):
    features, padded, reversed_band, mixed_rows, source = saved_state
    tap_count = weights.shape[0]
    kernel_width = reversed_band.shape[2]
    token_count, channels = incoming.shape
    edge_rows = tap_count - 1
    dense_float = dense_part.astype(jnp.float32)
    mixed_grad = (dense_float * features[0]).astype(jnp.bfloat16)
    after_grad = passed_along(mixed_grad[: kernel_width - 1], "seq", -1)
    trailing_grad = jnp.concatenate(
        [mixed_grad, after_grad, jnp.zeros((1, channels), jnp.bfloat16)], axis=0
    )

    def middle(operand):
        product_grad = long_backward(operand, reversed_band, groups)
        query_grad = dense_float * mixed_rows
        return (
            jnp.stack([query_grad, product_grad * features[2], product_grad * features[1]]),
            product_grad,
        )

    def middle_skipped(operand):
        return (
            jnp.zeros((3, token_count, channels), jnp.float32),
            jnp.zeros((token_count, channels), jnp.float32),
        )

    feature_grads, product_grad = lax.cond(active, middle, middle_skipped, trailing_grad)
    head_zeros = jnp.zeros((3, edge_rows, channels), jnp.float32)
    partial_sums = spread_back(
        jnp.concatenate([head_zeros, feature_grads[:, :edge_rows]], axis=1), weights
    )
    overflow = passed_along(partial_sums.astype(jnp.bfloat16), "seq", -1).astype(partial_sums.dtype)

    def finish(operands):
        grads, spill = operands
        trailing = jnp.concatenate([grads, head_zeros], axis=1)
        tail_rows = jnp.concatenate(
            [jnp.zeros((token_count - edge_rows, channels), jnp.float32), spill], axis=0
        )
        total = incoming.astype(jnp.float32) + spread_back(trailing, weights) + tail_rows
        return total.astype(jnp.bfloat16)

    def finish_skipped(operands):
        return jnp.zeros((token_count, channels), jnp.bfloat16)

    return (lax.cond(active, finish, finish_skipped, (feature_grads, overflow)), product_grad)


def per_device(layer_inputs, out_grad, short_weights, long_filters, out_weights):
    sections = lax.axis_size("pipe")
    section_index = lax.axis_index("pipe")
    weights = short_weights[0].astype(jnp.float32)
    filters = long_filters[0]
    groups = filters.shape[0]
    saved_state = recompute(layer_inputs[0], weights, filters)
    features, padded, reversed_band, mixed_rows, source = saved_state
    columns = lax.all_gather(out_weights[0], "seq", axis=1, tiled=True)
    incoming = out_grad
    input_result = jnp.zeros_like(out_grad)
    dense_kept = jnp.zeros(out_grad.shape, jnp.bfloat16)
    product_kept = jnp.zeros(out_grad.shape, jnp.float32)
    for step_index in range(sections):
        active = section_index == sections - 1 - step_index
        dense_part = dense_grad(incoming, columns, active)
        input_grad, product_grad = backward(
            saved_state, incoming, dense_part, weights, groups, active
        )
        input_result = jnp.where(active, input_grad, input_result)
        dense_kept = jnp.where(active, dense_part, dense_kept)
        product_kept = jnp.where(active, product_grad, product_kept)
        if step_index + 1 < sections:
            incoming = passed_along(input_grad, "pipe", -1)
    dense_float = dense_kept.astype(jnp.float32)
    mixed_grad = (dense_float * features[0]).astype(jnp.bfloat16)
    feature_grads = jnp.stack(
        [dense_float * mixed_rows, product_kept * features[2], product_kept * features[1]]
    )
    short_local = weight_grads(feature_grads, source)
    long_local = filter_grads(mixed_grad, padded, groups)
    short_result, long_result = (
        lax.psum(short_local.astype(jnp.bfloat16), "seq").astype(jnp.float32),
        lax.psum(long_local.astype(jnp.bfloat16), "seq").astype(jnp.float32),
    )
    return (input_result[None], short_result[None], long_result[None])


def solution(mesh):
    in_specs = (
        P("pipe", ("seq", "tp"), None),
        P("seq", "tp"),
        P("pipe", None, None, "tp"),
        P("pipe", "tp", None),
        P("pipe", "tp", "seq"),
    )
    out_specs = (P("pipe", "seq", "tp"), P("pipe", None, None, "tp"), P("pipe", "tp", None))
    return jax.shard_map(
        per_device, mesh=mesh, in_specs=in_specs, out_specs=out_specs, check_vma=False
    )
```

profile of v0, /device:TPU:32, one launch (start us, length us, event | category | flops | bytes accessed | tf_op | source)
XLA Modules:
  0.0 1389.2 jit_solution(17497464794075836733)
XLA Ops:
  88.4 68.1 %all-gather.27.cloned.1.call-done = bf16[1,2048,4096]{2,1,0:T(8,128)(2,1)} async-done(((bf16[1,2048,256]{2,1,0:T(8,128)(2,1)}), bf16[1,2048,4096]{2,1,0:T(8,128)(2,1)}) %all-gather.27.cloned.1.call-update) | async-done | bytes 16777232 | tf_op jit(solution)/shard_map/all_gather | solution.py:186
  235.9 56.1 %all-gather.13.cloned.1.call-done = bf16[128,4096]{1,0:T(8,128)(2,1)} async-done(((bf16[128,2048]{1,0:T(8,128)(2,1)}), bf16[128,4096]{1,0:T(8,128)(2,1)}) %all-gather.13.cloned.1.call-update) | async-done | bytes 1048592 | tf_op jit(solution)/shard_map/all_gather | solution.py:120
  298.1 14.7 %collective-permute-done.5 = bf16[127,2048]{0,1:T(8,128)(2,1)S(1)} collective-permute-done((bf16[127,2048]{0,1:T(8,128)(2,1)S(1)}, bf16[127,2048]{0,1:T(8,128)(2,1)S(1)}, u32[]{:S(2)}, u32[]{:S(2)}) %collective-permute-start.5) | collective-permute-done | bytes 520224 | tf_op jit(solution)/shard_map/ppermute | solution.py:10
  361.0 63.3 %all-gather.15.cloned.1.call-done = bf16[128,4096]{1,0:T(8,128)(2,1)} async-done(((bf16[128,2048]{1,0:T(8,128)(2,1)}), bf16[128,4096]{1,0:T(8,128)(2,1)}) %all-gather.15.cloned.1.call-update) | async-done | bytes 1048592 | tf_op jit(solution)/shard_map/all_gather | solution.py:120
  430.1 14.7 %collective-permute-done.8 = bf16[127,2048]{0,1:T(8,128)(2,1)S(1)} collective-permute-done((bf16[127,2048]{0,1:T(8,128)(2,1)S(1)}, bf16[127,2048]{0,1:T(8,128)(2,1)S(1)}, u32[]{:S(2)}, u32[]{:S(2)}) %collective-permute-start.8) | collective-permute-done | bytes 520224 | tf_op jit(solution)/shard_map/ppermute | solution.py:10
  462.6 13.9 %collective-permute-done.9 = bf16[6,2048]{0,1:T(8,128)(2,1)S(1)} collective-permute-done((bf16[6,2048]{0,1:T(8,128)(2,1)S(1)}, bf16[6,2048]{0,1:T(8,128)(2,1)S(1)}, u32[]{:S(2)}, u32[]{:S(2)}) %collective-permute-start.9) | collective-permute-done | bytes 24608 | tf_op jit(solution)/shard_map/ppermute | solution.py:10
  493.1 64.1 %all-gather.17.cloned.1.call-done = bf16[128,4096]{1,0:T(8,128)(2,1)} async-done(((bf16[128,2048]{1,0:T(8,128)(2,1)}), bf16[128,4096]{1,0:T(8,128)(2,1)}) %all-gather.17.cloned.1.call-update) | async-done | bytes 1048592 | tf_op jit(solution)/shard_map/all_gather | solution.py:120
  562.9 14.7 %collective-permute-done.11 = bf16[127,2048]{0,1:T(8,128)(2,1)S(1)} collective-permute-done((bf16[127,2048]{0,1:T(8,128)(2,1)S(1)}, bf16[127,2048]{0,1:T(8,128)(2,1)S(1)}, u32[]{:S(2)}, u32[]{:S(2)}) %collective-permute-start.11) | collective-permute-done | bytes 520224 | tf_op jit(solution)/shard_map/ppermute | solution.py:10
  595.6 13.9 %collective-permute-done.12 = bf16[6,2048]{0,1:T(8,128)(2,1)S(1)} collective-permute-done((bf16[6,2048]{0,1:T(8,128)(2,1)S(1)}, bf16[6,2048]{0,1:T(8,128)(2,1)S(1)}, u32[]{:S(2)}, u32[]{:S(2)}) %collective-permute-start.12) | collective-permute-done | bytes 24608 | tf_op jit(solution)/shard_map/ppermute | solution.py:10
  626.1 65.0 %all-gather.19.cloned.1.call-done = bf16[128,4096]{1,0:T(8,128)(2,1)} async-done(((bf16[128,2048]{1,0:T(8,128)(2,1)}), bf16[128,4096]{1,0:T(8,128)(2,1)}) %all-gather.19.cloned.1.call-update) | async-done | bytes 1048592 | tf_op jit(solution)/shard_map/all_gather | solution.py:120
  696.9 14.7 %collective-permute-done.14 = bf16[127,2048]{0,1:T(8,128)(2,1)S(1)} collective-permute-done((bf16[127,2048]{0,1:T(8,128)(2,1)S(1)}, bf16[127,2048]{0,1:T(8,128)(2,1)S(1)}, u32[]{:S(2)}, u32[]{:S(2)}) %collective-permute-start.14) | collective-permute-done | bytes 520224 | tf_op jit(solution)/shard_map/ppermute | solution.py:10
  729.2 13.9 %collective-permute-done.15 = bf16[6,2048]{0,1:T(8,128)(2,1)S(1)} collective-permute-done((bf16[6,2048]{0,1:T(8,128)(2,1)S(1)}, bf16[6,2048]{0,1:T(8,128)(2,1)S(1)}, u32[]{:S(2)}, u32[]{:S(2)}) %collective-permute-start.15) | collective-permute-done | bytes 24608 | tf_op jit(solution)/shard_map/ppermute | solution.py:10
  759.9 64.0 %all-gather.21.cloned.1.call-done = bf16[128,4096]{1,0:T(8,128)(2,1)} async-done(((bf16[128,2048]{1,0:T(8,128)(2,1)}), bf16[128,4096]{1,0:T(8,128)(2,1)}) %all-gather.21.cloned.1.call-update) | async-done | bytes 1048592 | tf_op jit(solution)/shard_map/all_gather | solution.py:120
  829.6 14.7 %collective-permute-done.17 = bf16[127,2048]{0,1:T(8,128)(2,1)S(1)} collective-permute-done((bf16[127,2048]{0,1:T(8,128)(2,1)S(1)}, bf16[127,2048]{0,1:T(8,128)(2,1)S(1)}, u32[]{:S(2)}, u32[]{:S(2)}) %collective-permute-start.17) | collective-permute-done | bytes 520224 | tf_op jit(solution)/shard_map/ppermute | solution.py:10
  880.8 57.0 %collective-permute-done.19 = bf16[128,2048]{1,0:T(8,128)(2,1)} collective-permute-done((bf16[128,2048]{1,0:T(8,128)(2,1)}, bf16[128,2048]{1,0:T(8,128)(2,1)}, u32[]{:S(2)}, u32[]{:S(2)}) %collective-permute-start.19) | collective-permute-done | bytes 524320 | tf_op jit(solution)/shard_map/ppermute | solution.py:10
  937.8 16.7 %all-gather.23.cloned.1.call-done = bf16[128,4096]{1,0:T(8,128)(2,1)} async-done(((bf16[128,2048]{1,0:T(8,128)(2,1)}), bf16[128,4096]{1,0:T(8,128)(2,1)}) %all-gather.23.cloned.1.call-update) | async-done | bytes 1048592 | tf_op jit(solution)/shard_map/all_gather | solution.py:120
  954.5 17.2 %conditional.42 = (f32[128,2048]{1,0:T(8,128)}, f32[128,2048]{0,1:T(8,128)}, bf16[128,2048]{0,1:T(8,128)(2,1)}) conditional(s32[]{:T(128)} %convert_element_type.283, () %tuple.255, (bf16[128,4096]{1,0:T(8,128)(2,1)}, bf16[2048,4096]{1,0:T(8,128)(2,1)}) %tuple.637), branch_computations={%region_115.116_spmd, %region_116.117_spmd} | conditional | flops 2148007936 | bytes 22020120 | solution.py:121
  974.4 14.7 %collective-permute-done.20 = bf16[127,2048]{0,1:T(8,128)(2,1)S(1)} collective-permute-done((bf16[127,2048]{0,1:T(8,128)(2,1)S(1)}, bf16[127,2048]{0,1:T(8,128)(2,1)S(1)}, u32[]{:S(2)}, u32[]{:S(2)}) %collective-permute-start.20) | collective-permute-done | bytes 520224 | tf_op jit(solution)/shard_map/ppermute | solution.py:10
  1017.9 13.9 %collective-permute-done.21 = bf16[6,2048]{0,1:T(8,128)(2,1)S(1)} collective-permute-done((bf16[6,2048]{0,1:T(8,128)(2,1)S(1)}, bf16[6,2048]{0,1:T(8,128)(2,1)S(1)}, u32[]{:S(2)}, u32[]{:S(2)}) %collective-permute-start.21) | collective-permute-done | bytes 24608 | tf_op jit(solution)/shard_map/ppermute | solution.py:10
  1032.9 20.9 %conditional.44 = (bf16[128,2048]{1,0:T(8,128)(2,1)}) conditional(s32[]{:T(128)} %convert_element_type.283, () %tuple.217, (bf16[128,2048]{1,0:T(8,128)(2,1)}, f32[7,3,2048]{2,1,0:T(4,128)S(1)}, f32[3,128,2048]{1,2,0:T(8,128)}, f32[6,2048]{0,1:T(8,128)}) %tuple.258), branch_computations={%region_125.126_spmd, %region_126.134_spmd} | conditional | flops 11796480 | bytes 26026020 | solution.py:175
  1099.4 17.8 %copy.274 = f32[128,128,256]{0,2,1:T(8,128)} copy(f32[128,128,256]{2,1,0:T(8,128)} %fusion.30) | data formatting | bytes 33554432 | tf_op jit(solution)/shard_map/reshape | solution.py:29
  1130.5 17.5 %reshape.203 = f32[128,128,257]{0,2,1:T(8,128)} reshape(f32[128,32896]{0,1:T(8,128)} %pad.28) | data formatting | bytes 33685504 | tf_op jit(solution)/shard_map/reshape | solution.py:31
  1158.1 77.1 %psum.15 = bf16[1,128,128]{1,2,0:T(8,128)(2,1)} all-reduce(bf16[1,128,128]{1,2,0:T(8,128)(2,1)} %bitcast.399), channel_id=1, replica_groups=mesh['pipe'=8,'seq'=16,'tp'=2] {'seq'}, use_global_device_ids=true, to_apply=%region_162.163 | all-reduce | flops 16384 | bytes 65536 | tf_op jit(solution)/shard_map/psum | solution.py:211
  1280.5 99.8 %all-reduce.27.cloned.1.call-done = bf16[1,7,3,2048]{3,1,2,0:T(8,128)(2,1)} async-done(((bf16[1,7,3,2048]{3,1,2,0:T(8,128)(2,1)}), bf16[1,7,3,2048]{3,1,2,0:T(8,128)(2,1)}) %all-reduce.27.cloned.1.call-update) | async-done | bytes 86032 | tf_op jit(solution)/shard_map/psum | solution.py:210
  (307 shorter events, 618.4 us)
Async XLA Ops:
  7.2 81.3 %all-gather.11.cloned.1.call-start = ((), (), s32[]{:S(2)}) async-start(), calls=%async_computation.1 | async-start | bytes 1572864 | tf_op jit(solution)/shard_map/all_gather | solution.py:120
  7.9 148.7 %all-gather.27.cloned.1.call-start = ((), (), s32[]{:S(2)}) async-start(), calls=%async_computation.10 | async-start | bytes 17825792 | tf_op jit(solution)/shard_map/all_gather | solution.py:186
  8.7 283.3 %all-gather.13.cloned.1.call-start = ((), (), s32[]{:S(2)}) async-start(), calls=%async_computation.2 | async-start | bytes 1572864 | tf_op jit(solution)/shard_map/all_gather | solution.py:120
  14.5 47.9 %collective-permute-start = (bf16[6,2048]{1,0:T(8,128)(2,1)S(1)}, bf16[6,2048]{1,0:T(8,128)(2,1)S(1)}, u32[]{:S(2)}, u32[]{:S(2)}) collective-permute-start(bf16[6,2048]{1,0:T(8,128)(2,1)S(1)} %slice.757), channel_id=1, source_target_pairs={{0,2},{2,4},{4,6},{6,8},{8,10},{10,12},{12,14},{14,16},{16,18},{18... | collective-permute-start | bytes 73736 | tf_op jit(solution)/shard_map/ppermute | solution.py:10
  235.8 188.6 %all-gather.15.cloned.1.call-start = ((), (), s32[]{:S(2)}) async-start(), calls=%async_computation.3 | async-start | bytes 1572864 | tf_op jit(solution)/shard_map/all_gather | solution.py:120
  296.8 16.0 %collective-permute-start.5 = (bf16[127,2048]{0,1:T(8,128)(2,1)S(1)}, bf16[127,2048]{0,1:T(8,128)(2,1)S(1)}, u32[]{:S(2)}, u32[]{:S(2)}) collective-permute-start(bf16[127,2048]{0,1:T(8,128)(2,1)S(1)} %bitcast.392), channel_id=1, source_target_pairs={{2,0},{4,2},{6,4},{8,6},{10,8},{12,10},{14,12},{16,14},{18,16},{20... | collective-permute-start | bytes 1560584 | tf_op jit(solution)/shard_map/ppermute | solution.py:10
  361.0 196.2 %all-gather.17.cloned.1.call-start = ((), (), s32[]{:S(2)}) async-start(), calls=%async_computation.4 | async-start | bytes 1572864 | tf_op jit(solution)/shard_map/all_gather | solution.py:120
  428.8 16.0 %collective-permute-start.8 = (bf16[127,2048]{0,1:T(8,128)(2,1)S(1)}, bf16[127,2048]{0,1:T(8,128)(2,1)S(1)}, u32[]{:S(2)}, u32[]{:S(2)}) collective-permute-start(bf16[127,2048]{0,1:T(8,128)(2,1)S(1)} %bitcast.393), channel_id=1, source_target_pairs={{2,0},{4,2},{6,4},{8,6},{10,8},{12,10},{14,12},{16,14},{18,16},{20... | collective-permute-start | bytes 1560584 | tf_op jit(solution)/shard_map/ppermute | solution.py:10
  461.3 15.2 %collective-permute-start.9 = (bf16[6,2048]{0,1:T(8,128)(2,1)S(1)}, bf16[6,2048]{0,1:T(8,128)(2,1)S(1)}, u32[]{:S(2)}, u32[]{:S(2)}) collective-permute-start(bf16[6,2048]{0,1:T(8,128)(2,1)S(1)} %add_convert_fusion.13), channel_id=1, source_target_pairs={{2,0},{4,2},{6,4},{8,6},{10,8},{12,10},{14,12},{16,14},{18,16},{20... | collective-permute-start | bytes 73736 | tf_op jit(solution)/shard_map/ppermute | solution.py:10
  493.0 198.1 %all-gather.19.cloned.1.call-start = ((), (), s32[]{:S(2)}) async-start(), calls=%async_computation.5 | async-start | bytes 1572864 | tf_op jit(solution)/shard_map/all_gather | solution.py:120
  561.6 16.0 %collective-permute-start.11 = (bf16[127,2048]{0,1:T(8,128)(2,1)S(1)}, bf16[127,2048]{0,1:T(8,128)(2,1)S(1)}, u32[]{:S(2)}, u32[]{:S(2)}) collective-permute-start(bf16[127,2048]{0,1:T(8,128)(2,1)S(1)} %bitcast.394), channel_id=1, source_target_pairs={{2,0},{4,2},{6,4},{8,6},{10,8},{12,10},{14,12},{16,14},{18,16},{20... | collective-permute-start | bytes 1560584 | tf_op jit(solution)/shard_map/ppermute | solution.py:10
  594.3 15.2 %collective-permute-start.12 = (bf16[6,2048]{0,1:T(8,128)(2,1)S(1)}, bf16[6,2048]{0,1:T(8,128)(2,1)S(1)}, u32[]{:S(2)}, u32[]{:S(2)}) collective-permute-start(bf16[6,2048]{0,1:T(8,128)(2,1)S(1)} %add_convert_fusion.12), channel_id=1, source_target_pairs={{2,0},{4,2},{6,4},{8,6},{10,8},{12,10},{14,12},{16,14},{18,16},{20... | collective-permute-start | bytes 73736 | tf_op jit(solution)/shard_map/ppermute | solution.py:10
  626.1 197.9 %all-gather.21.cloned.1.call-start = ((), (), s32[]{:S(2)}) async-start(), calls=%async_computation.6 | async-start | bytes 1572864 | tf_op jit(solution)/shard_map/all_gather | solution.py:120
  695.6 16.0 %collective-permute-start.14 = (bf16[127,2048]{0,1:T(8,128)(2,1)S(1)}, bf16[127,2048]{0,1:T(8,128)(2,1)S(1)}, u32[]{:S(2)}, u32[]{:S(2)}) collective-permute-start(bf16[127,2048]{0,1:T(8,128)(2,1)S(1)} %bitcast.395), channel_id=1, source_target_pairs={{2,0},{4,2},{6,4},{8,6},{10,8},{12,10},{14,12},{16,14},{18,16},{20... | collective-permute-start | bytes 1560584 | tf_op jit(solution)/shard_map/ppermute | solution.py:10
  727.9 15.2 %collective-permute-start.15 = (bf16[6,2048]{0,1:T(8,128)(2,1)S(1)}, bf16[6,2048]{0,1:T(8,128)(2,1)S(1)}, u32[]{:S(2)}, u32[]{:S(2)}) collective-permute-start(bf16[6,2048]{0,1:T(8,128)(2,1)S(1)} %add_convert_fusion.11), channel_id=1, source_target_pairs={{2,0},{4,2},{6,4},{8,6},{10,8},{12,10},{14,12},{16,14},{18,16},{20... | collective-permute-start | bytes 73736 | tf_op jit(solution)/shard_map/ppermute | solution.py:10
  759.9 194.7 %all-gather.23.cloned.1.call-start = ((), (), s32[]{:S(2)}) async-start(), calls=%async_computation.7 | async-start | bytes 1572864 | tf_op jit(solution)/shard_map/all_gather | solution.py:120
  828.3 16.0 %collective-permute-start.17 = (bf16[127,2048]{0,1:T(8,128)(2,1)S(1)}, bf16[127,2048]{0,1:T(8,128)(2,1)S(1)}, u32[]{:S(2)}, u32[]{:S(2)}) collective-permute-start(bf16[127,2048]{0,1:T(8,128)(2,1)S(1)} %bitcast.396), channel_id=1, source_target_pairs={{2,0},{4,2},{6,4},{8,6},{10,8},{12,10},{14,12},{16,14},{18,16},{20... | collective-permute-start | bytes 1560584 | tf_op jit(solution)/shard_map/ppermute | solution.py:10
  861.0 15.2 %collective-permute-start.18 = (bf16[6,2048]{0,1:T(8,128)(2,1)S(1)}, bf16[6,2048]{0,1:T(8,128)(2,1)S(1)}, u32[]{:S(2)}, u32[]{:S(2)}) collective-permute-start(bf16[6,2048]{0,1:T(8,128)(2,1)S(1)} %add_convert_fusion.10), channel_id=1, source_target_pairs={{2,0},{4,2},{6,4},{8,6},{10,8},{12,10},{14,12},{16,14},{18,16},{20... | collective-permute-start | bytes 73736 | tf_op jit(solution)/shard_map/ppermute | solution.py:10
  878.1 59.6 %collective-permute-start.19 = (bf16[128,2048]{1,0:T(8,128)(2,1)}, bf16[128,2048]{1,0:T(8,128)(2,1)}, u32[]{:S(2)}, u32[]{:S(2)}) collective-permute-start(bf16[128,2048]{1,0:T(8,128)(2,1)} %get-tuple-element.1092), channel_id=1, source_target_pairs={{32,0},{64,32},{96,64},{128,96},{160,128},{192,160},{224,192},{33,... | collective-permute-start | bytes 1572872 | tf_op jit(solution)/shard_map/ppermute | solution.py:10
  937.8 146.2 %all-gather.25.cloned.1.call-start = ((), (), s32[]{:S(2)}) async-start(), calls=%async_computation.8 | async-start | bytes 1572864 | tf_op jit(solution)/shard_map/all_gather | solution.py:120
  973.1 16.0 %collective-permute-start.20 = (bf16[127,2048]{0,1:T(8,128)(2,1)S(1)}, bf16[127,2048]{0,1:T(8,128)(2,1)S(1)}, u32[]{:S(2)}, u32[]{:S(2)}) collective-permute-start(bf16[127,2048]{0,1:T(8,128)(2,1)S(1)} %bitcast.397), channel_id=1, source_target_pairs={{2,0},{4,2},{6,4},{8,6},{10,8},{12,10},{14,12},{16,14},{18,16},{20... | collective-permute-start | bytes 1560584 | tf_op jit(solution)/shard_map/ppermute | solution.py:10
  1016.6 15.2 %collective-permute-start.21 = (bf16[6,2048]{0,1:T(8,128)(2,1)S(1)}, bf16[6,2048]{0,1:T(8,128)(2,1)S(1)}, u32[]{:S(2)}, u32[]{:S(2)}) collective-permute-start(bf16[6,2048]{0,1:T(8,128)(2,1)S(1)} %add_convert_fusion.9), channel_id=1, source_target_pairs={{2,0},{4,2},{6,4},{8,6},{10,8},{12,10},{14,12},{16,14},{18,16},{20... | collective-permute-start | bytes 73736 | tf_op jit(solution)/shard_map/ppermute | solution.py:10
  1068.4 311.9 %all-reduce.27.cloned.1.call-start = ((), (), s32[]{:S(2)}) async-start(), calls=%async_computation.9 | async-start | bytes 196608 | tf_op jit(solution)/shard_map/psum | solution.py:210
  1090.0 149.2 %collective-permute-start.23 = (bf16[127,2048]{0,1:T(8,128)(2,1)}, bf16[127,2048]{0,1:T(8,128)(2,1)}, u32[]{:S(2)}, u32[]{:S(2)}) collective-permute-start(bf16[127,2048]{0,1:T(8,128)(2,1)} %bitcast.351), channel_id=1, source_target_pairs={{2,0},{4,2},{6,4},{8,6},{10,8},{12,10},{14,12},{16,14},{18,16},{20... | collective-permute-start | bytes 1560584 | tf_op jit(solution)/shard_map/ppermute | solution.py:10
  (41 other events, 276.8 us)
Sparse Core Ops, SparseCore 0:
  9.8 16.9 all-gather.10
  29.2 127.3 all-gather.26
  235.9 55.9 all-gather.12
  361.1 63.2 all-gather.14
  493.1 63.9 all-gather.16
  626.2 64.8 all-gather.18
  760.0 63.8 all-gather.20
  937.9 16.6 all-gather.22
  1068.5 15.4 all-gather.24
  1268.5 111.7 all-reduce.26
where the time goes:
time: 1400 us; the launch traced here: 1390 us
  waiting for transfers between devices  826 us (59%)
  local copies, waits for them, and re-layouts  195 us (14%)
  other arithmetic  189 us (14%)
  blocking collectives  81.3 us (6%)
  starting transfers between devices  45.8 us (3%)
  matrix products  32.7 us (2%)
  between operations  15.6 us (1%)
    all_gather x8, waiting for transfers between devices, dense_grad(): piece = lax.all_gather(incoming, 'tp', axis=1, tiled=True)  330 us
    ppermute x25, waiting for transfers between devices, passed_along(): return lax.ppermute(array, axis, pairs)  327 us
    psum x1, waiting for transfers between devices, per_device(): lax.psum(short_local.astype(jnp.bfloat16), 'seq').astype(jnp.float32)  99.8 us
    reduce_sum x10, other arithmetic, spread_back(): jnp.sum(weights[offset][:, None, :] * feature_grads[:, offset:offset + ro...  88.6 us
    psum x1, blocking collectives, per_device(): lax.psum(long_local.astype(jnp.bfloat16), 'seq').astype(jnp.float32)  77.1 us
    all_gather x1, waiting for transfers between devices, per_device(): columns = lax.all_gather(out_weights[0], 'seq', axis=1, tiled=True)  68.1 us
    another operation x46, local copies, waits for them, and re-layouts  50.6 us
    ppermute x25, starting transfers between devices, passed_along(): return lax.ppermute(array, axis, pairs)  45.4 us
  transfers between devices with their start and end apart: 35, of which 32 were waited for; matrix products, arithmetic and copies ran while one was open for 12% of the time, Pallas kernels for 0%

commit v1 on v0

--- a/solution.py
+++ b/solution.py
@@ -2,6 +2,7 @@
 import jax.numpy as jnp
 from jax import lax
 from jax.sharding import PartitionSpec as P
+from jax.lax import all_to_all, axis_size
 
 
 def passed_along(array, axis, by):
@@ -183,7 +184,10 @@
     groups = filters.shape[0]
     saved_state = recompute(layer_inputs[0], weights, filters)
     features, padded, reversed_band, mixed_rows, source = saved_state
-    columns = lax.all_gather(out_weights[0], "seq", axis=1, tiled=True)
+    fill_steps_all_here = lambda local_values, net_axis, pos_dim: jnp.concatenate(
+        all_to_all(jnp.stack(axis_size(net_axis) * [local_values]), net_axis, 0, 0), axis=pos_dim
+    )
+    columns = fill_steps_all_here(out_weights[0], "seq", 1)
     incoming = out_grad
     input_result = jnp.zeros_like(out_grad)
     dense_kept = jnp.zeros(out_grad.shape, jnp.bfloat16)

time: 1400 us -> 1560 us (1.11)
  waiting for transfers between devices: 826 us -> 954 us
  local copies, waits for them, and re-layouts: 195 us -> 223 us
    all_to_all x0 -> x1, waiting for transfers between devices: none -> 123 us  [per_device(): all_to_all(jnp.stack(axis_size(net_axis) * [local_values]), net_axis, 0, 0)]
    ppermute x25, waiting for transfers between devices: 327 us -> 421 us  [passed_along(): return lax.ppermute(array, axis, pairs)]
    all_gather x1 -> x0, waiting for transfers between devices: 68.1 us -> none  [per_device(): columns = lax.all_gather(out_weights[0], 'seq', axis=1, tiled=True)]
    all_to_all x0 -> x1, local copies, waits for them, and re-layouts: none -> 21.6 us  [per_device(): all_to_all(jnp.stack(axis_size(net_axis) * [local_values]), net_axis, 0, 0)]
    all_gather x8, waiting for transfers between devices: 330 us -> 313 us  [dense_grad(): piece = lax.all_gather(incoming, 'tp', axis=1, tiled=True)]
    another operation x46 -> x47, local copies, waits for them, and re-layouts: 50.6 us -> 56.4 us
  transfers between devices with their start and end apart: 35 -> 35, of which waited for: 32 -> 33; matrix products, arithmetic and copies ran while one was open for 12% -> 12% of each run, Pallas kernels for 0% -> 0%
where the time goes in v1:
time: 1560 us; the launch traced here: 1550 us
  waiting for transfers between devices  954 us (61%)
  local copies, waits for them, and re-layouts  223 us (14%)
  other arithmetic  189 us (12%)
  blocking collectives  81.3 us (5%)
  starting transfers between devices  57.8 us (4%)
  matrix products  29.5 us (2%)
    ppermute x25, waiting for transfers between devices, passed_along(): return lax.ppermute(array, axis, pairs)  421 us
    all_gather x8, waiting for transfers between devices, dense_grad(): piece = lax.all_gather(incoming, 'tp', axis=1, tiled=True)  313 us
    all_to_all x1, waiting for transfers between devices, per_device(): all_to_all(jnp.stack(axis_size(net_axis) * [local_values]), net_axis, 0, 0)  123 us
    psum x1, waiting for transfers between devices, per_device(): lax.psum(short_local.astype(jnp.bfloat16), 'seq').astype(jnp.float32)  96.5 us
    reduce_sum x10, other arithmetic, spread_back(): jnp.sum(weights[offset][:, None, :] * feature_grads[:, offset:offset + ro...  88.7 us
    psum x1, blocking collectives, per_device(): lax.psum(long_local.astype(jnp.bfloat16), 'seq').astype(jnp.float32)  77.1 us
    another operation x46, local copies, waits for them, and re-layouts  50.5 us
    ppermute x25, starting transfers between devices, passed_along(): return lax.ppermute(array, axis, pairs)  50 us
  transfers between devices with their start and end apart: 35, of which 33 were waited for; matrix products, arithmetic and copies ran while one was open for 12% of the time, Pallas kernels for 0%

profile of v1, /device:TPU:32, one launch (start us, length us, event | category | flops | bytes accessed | tf_op | source)
XLA Modules:
  0.0 1551.5 jit_solution(1414279517346782488)
XLA Ops:
  75.1 98.5 %collective-permute-done = bf16[6,2048]{1,0:T(8,128)(2,1)S(1)} collective-permute-done((bf16[6,2048]{1,0:T(8,128)(2,1)S(1)}, bf16[6,2048]{1,0:T(8,128)(2,1)S(1)}, u32[]{:S(2)}, u32[]{:S(2)}) %collective-permute-start) | collective-permute-done | bytes 24608 | tf_op jit(solution)/shard_map/ppermute | solution.py:11
  199.6 122.6 %all-to-all-done = bf16[16,2048,256]{2,1,0:T(8,128)(2,1)} async-done(((bf16[16,2048,256]{2,1,0:T(8,128)(2,1)}), bf16[16,2048,256]{2,1,0:T(8,128)(2,1)}, u32[]{:S(2)}, u32[]{:S(2)}) %all-to-all-start) | async-done | bytes 16777248 | tf_op jit(solution)/shard_map/all_to_all | solution.py:188
  322.1 21.6 %copy.274 = bf16[16,2048,256]{1,2,0:T(8,128)(2,1)} copy(bf16[16,2048,256]{2,1,0:T(8,128)(2,1)} %all-to-all-done) | data formatting | bytes 33554432 | tf_op jit(solution)/shard_map/all_to_all | solution.py:188
  426.4 53.1 %all-gather.11.cloned.1.call-done = bf16[128,4096]{1,0:T(8,128)(2,1)} async-done(((bf16[128,2048]{1,0:T(8,128)(2,1)}), bf16[128,4096]{1,0:T(8,128)(2,1)}) %all-gather.11.cloned.1.call-update) | async-done | bytes 1048592 | tf_op jit(solution)/shard_map/all_gather | solution.py:121
  485.4 14.7 collective-permute-done.5
  517.6 13.9 collective-permute-done.6
  548.1 59.9 %all-gather.13.cloned.1.call-done = bf16[128,4096]{1,0:T(8,128)(2,1)} async-done(((bf16[128,2048]{1,0:T(8,128)(2,1)}), bf16[128,4096]{1,0:T(8,128)(2,1)}) %all-gather.13.cloned.1.call-update) | async-done | bytes 1048592 | tf_op jit(solution)/shard_map/all_gather | solution.py:121
  613.9 14.7 collective-permute-done.8
  676.7 60.7 %all-gather.15.cloned.1.call-done = bf16[128,4096]{1,0:T(8,128)(2,1)} async-done(((bf16[128,2048]{1,0:T(8,128)(2,1)}), bf16[128,4096]{1,0:T(8,128)(2,1)}) %all-gather.15.cloned.1.call-update) | async-done | bytes 1048592 | tf_op jit(solution)/shard_map/all_gather | solution.py:121
  743.5 14.7 collective-permute-done.11
  775.8 13.9 collective-permute-done.12
  806.3 61.5 %all-gather.17.cloned.1.call-done = bf16[128,4096]{1,0:T(8,128)(2,1)} async-done(((bf16[128,2048]{1,0:T(8,128)(2,1)}), bf16[128,4096]{1,0:T(8,128)(2,1)}) %all-gather.17.cloned.1.call-update) | async-done | bytes 1048592 | tf_op jit(solution)/shard_map/all_gather | solution.py:121
  873.6 14.7 collective-permute-done.14
  936.5 60.6 %all-gather.19.cloned.1.call-done = bf16[128,4096]{1,0:T(8,128)(2,1)} async-done(((bf16[128,2048]{1,0:T(8,128)(2,1)}), bf16[128,4096]{1,0:T(8,128)(2,1)}) %all-gather.19.cloned.1.call-update) | async-done | bytes 1048592 | tf_op jit(solution)/shard_map/all_gather | solution.py:121
  1002.9 14.7 collective-permute-done.17
  1053.7 53.6 %collective-permute-done.19 = bf16[128,2048]{1,0:T(8,128)(2,1)} collective-permute-done((bf16[128,2048]{1,0:T(8,128)(2,1)}, bf16[128,2048]{1,0:T(8,128)(2,1)}, u32[]{:S(2)}, u32[]{:S(2)}) %collective-permute-start.19) | collective-permute-done | bytes 524320 | tf_op jit(solution)/shard_map/ppermute | solution.py:11
  1107.4 16.7 %all-gather.21.cloned.1.call-done = bf16[128,4096]{1,0:T(8,128)(2,1)} async-done(((bf16[128,2048]{1,0:T(8,128)(2,1)}), bf16[128,4096]{1,0:T(8,128)(2,1)}) %all-gather.21.cloned.1.call-update) | async-done | bytes 1048592 | tf_op jit(solution)/shard_map/all_gather | solution.py:121
  1124.1 14.4 conditional.42
  1141.1 14.7 collective-permute-done.20
  1199.3 20.9 %conditional.44 = (bf16[128,2048]{1,0:T(8,128)(2,1)}) conditional(s32[]{:T(128)} %convert_element_type.283, () %tuple.217, (bf16[128,2048]{1,0:T(8,128)(2,1)}, f32[7,3,2048]{2,1,0:T(4,128)S(1)}, f32[3,128,2048]{1,2,0:T(8,128)}, f32[6,2048]{0,1:T(8,128)}) %tuple.258), branch_computations={%region_125.126_spmd, %region_126.134_spmd} | conditional | flops 11796480 | bytes 26026020 | solution.py:176
  1265.5 17.8 %copy.355 = f32[128,128,256]{0,2,1:T(8,128)} copy(f32[128,128,256]{2,1,0:T(8,128)} %fusion.30) | data formatting | bytes 33554432 | tf_op jit(solution)/shard_map/reshape | solution.py:30
  1296.6 17.5 %reshape.212 = f32[128,128,257]{0,2,1:T(8,128)} reshape(f32[128,32896]{0,1:T(8,128)} %pad.28) | data formatting | bytes 33685504 | tf_op jit(solution)/shard_map/reshape | solution.py:32
  1324.2 77.1 %psum.15 = bf16[1,128,128]{1,2,0:T(8,128)(2,1)} all-reduce(bf16[1,128,128]{1,2,0:T(8,128)(2,1)} %bitcast.403), channel_id=1, replica_groups=mesh['pipe'=8,'seq'=16,'tp'=2] {'seq'}, use_global_device_ids=true, to_apply=%region_162.163 | all-reduce | flops 16384 | bytes 65536 | tf_op jit(solution)/shard_map/psum | solution.py:215
  1446.5 96.5 %all-reduce.27.cloned.1.call-done = bf16[1,7,3,2048]{3,1,2,0:T(8,128)(2,1)} async-done(((bf16[1,7,3,2048]{3,1,2,0:T(8,128)(2,1)}), bf16[1,7,3,2048]{3,1,2,0:T(8,128)(2,1)}) %all-reduce.27.cloned.1.call-update) | async-done | bytes 86032 | tf_op jit(solution)/shard_map/psum | solution.py:214
  (310 shorter events, 657.3 us)
Async XLA Ops:
  18.9 303.2 %all-to-all-start = ((bf16[16,2048,256]{2,1,0:T(8,128)(2,1)}), bf16[16,2048,256]{2,1,0:T(8,128)(2,1)}, u32[]{:S(2)}, u32[]{:S(2)}) async-start(bf16[16,2048,256]{2,1,0:T(8,128)(2,1)} %stack.111), calls=%async_computation | async-start | bytes 33554432 | tf_op jit(solution)/shard_map/all_to_all | solution.py:188
  26.1 317.7 %all-gather.9.cloned.1.call-start = ((), (), s32[]{:S(2)}) async-start(), calls=%async_computation.2 | async-start | bytes 1572864 | tf_op jit(solution)/shard_map/all_gather | solution.py:121
  26.9 452.6 %all-gather.11.cloned.1.call-start = ((), (), s32[]{:S(2)}) async-start(), calls=%async_computation.3 | async-start | bytes 1572864 | tf_op jit(solution)/shard_map/all_gather | solution.py:121
  26.9 146.7 %collective-permute-start = (bf16[6,2048]{1,0:T(8,128)(2,1)S(1)}, bf16[6,2048]{1,0:T(8,128)(2,1)S(1)}, u32[]{:S(2)}, u32[]{:S(2)}) collective-permute-start(bf16[6,2048]{1,0:T(8,128)(2,1)S(1)} %slice.757), channel_id=1, source_target_pairs={{0,2},{2,4},{4,6},{6,8},{8,10},{10,12},{12,14},{14,16},{16,18},{18... | collective-permute-start | bytes 73736 | tf_op jit(solution)/shard_map/ppermute | solution.py:11
  350.9 16.9 %collective-permute-start.1 = (bf16[127,2048]{0,1:T(8,128)(2,1)}, bf16[127,2048]{0,1:T(8,128)(2,1)}, u32[]{:S(2)}, u32[]{:S(2)}) collective-permute-start(bf16[127,2048]{0,1:T(8,128)(2,1)} %slice.773), channel_id=1, source_target_pairs={{0,2},{2,4},{4,6},{6,8},{8,10},{10,12},{12,14},{14,16},{16,18},{18... | collective-permute-start | bytes 1560584 | tf_op jit(solution)/shard_map/ppermute | solution.py:11
  426.3 181.7 %all-gather.13.cloned.1.call-start = ((), (), s32[]{:S(2)}) async-start(), calls=%async_computation.4 | async-start | bytes 1572864 | tf_op jit(solution)/shard_map/all_gather | solution.py:121
  484.1 16.0 %collective-permute-start.5 = (bf16[127,2048]{0,1:T(8,128)(2,1)S(1)}, bf16[127,2048]{0,1:T(8,128)(2,1)S(1)}, u32[]{:S(2)}, u32[]{:S(2)}) collective-permute-start(bf16[127,2048]{0,1:T(8,128)(2,1)S(1)} %bitcast.395), channel_id=1, source_target_pairs={{2,0},{4,2},{6,4},{8,6},{10,8},{12,10},{14,12},{16,14},{18,16},{20... | collective-permute-start | bytes 1560584 | tf_op jit(solution)/shard_map/ppermute | solution.py:11
  516.3 15.2 collective-permute-start.6
  548.1 189.4 %all-gather.15.cloned.1.call-start = ((), (), s32[]{:S(2)}) async-start(), calls=%async_computation.5 | async-start | bytes 1572864 | tf_op jit(solution)/shard_map/all_gather | solution.py:121
  612.6 16.0 %collective-permute-start.8 = (bf16[127,2048]{0,1:T(8,128)(2,1)S(1)}, bf16[127,2048]{0,1:T(8,128)(2,1)S(1)}, u32[]{:S(2)}, u32[]{:S(2)}) collective-permute-start(bf16[127,2048]{0,1:T(8,128)(2,1)S(1)} %bitcast.396), channel_id=1, source_target_pairs={{2,0},{4,2},{6,4},{8,6},{10,8},{12,10},{14,12},{16,14},{18,16},{20... | collective-permute-start | bytes 1560584 | tf_op jit(solution)/shard_map/ppermute | solution.py:11
  644.9 15.2 collective-permute-start.9
  676.7 191.1 %all-gather.17.cloned.1.call-start = ((), (), s32[]{:S(2)}) async-start(), calls=%async_computation.6 | async-start | bytes 1572864 | tf_op jit(solution)/shard_map/all_gather | solution.py:121
  742.2 16.0 %collective-permute-start.11 = (bf16[127,2048]{0,1:T(8,128)(2,1)S(1)}, bf16[127,2048]{0,1:T(8,128)(2,1)S(1)}, u32[]{:S(2)}, u32[]{:S(2)}) collective-permute-start(bf16[127,2048]{0,1:T(8,128)(2,1)S(1)} %bitcast.397), channel_id=1, source_target_pairs={{2,0},{4,2},{6,4},{8,6},{10,8},{12,10},{14,12},{16,14},{18,16},{20... | collective-permute-start | bytes 1560584 | tf_op jit(solution)/shard_map/ppermute | solution.py:11
  774.5 15.2 collective-permute-start.12
  806.2 190.8 %all-gather.19.cloned.1.call-start = ((), (), s32[]{:S(2)}) async-start(), calls=%async_computation.7 | async-start | bytes 1572864 | tf_op jit(solution)/shard_map/all_gather | solution.py:121
  872.3 16.0 %collective-permute-start.14 = (bf16[127,2048]{0,1:T(8,128)(2,1)S(1)}, bf16[127,2048]{0,1:T(8,128)(2,1)S(1)}, u32[]{:S(2)}, u32[]{:S(2)}) collective-permute-start(bf16[127,2048]{0,1:T(8,128)(2,1)S(1)} %bitcast.398), channel_id=1, source_target_pairs={{2,0},{4,2},{6,4},{8,6},{10,8},{12,10},{14,12},{16,14},{18,16},{20... | collective-permute-start | bytes 1560584 | tf_op jit(solution)/shard_map/ppermute | solution.py:11
  936.5 187.6 %all-gather.21.cloned.1.call-start = ((), (), s32[]{:S(2)}) async-start(), calls=%async_computation.8 | async-start | bytes 1572864 | tf_op jit(solution)/shard_map/all_gather | solution.py:121
  1001.6 16.0 %collective-permute-start.17 = (bf16[127,2048]{0,1:T(8,128)(2,1)S(1)}, bf16[127,2048]{0,1:T(8,128)(2,1)S(1)}, u32[]{:S(2)}, u32[]{:S(2)}) collective-permute-start(bf16[127,2048]{0,1:T(8,128)(2,1)S(1)} %bitcast.399), channel_id=1, source_target_pairs={{2,0},{4,2},{6,4},{8,6},{10,8},{12,10},{14,12},{16,14},{18,16},{20... | collective-permute-start | bytes 1560584 | tf_op jit(solution)/shard_map/ppermute | solution.py:11
  1051.0 56.3 %collective-permute-start.19 = (bf16[128,2048]{1,0:T(8,128)(2,1)}, bf16[128,2048]{1,0:T(8,128)(2,1)}, u32[]{:S(2)}, u32[]{:S(2)}) collective-permute-start(bf16[128,2048]{1,0:T(8,128)(2,1)} %get-tuple-element.1183), channel_id=1, source_target_pairs={{32,0},{64,32},{96,64},{128,96},{160,128},{192,160},{224,192},{33,... | collective-permute-start | bytes 1572872 | tf_op jit(solution)/shard_map/ppermute | solution.py:11
  1107.3 143.1 %all-gather.23.cloned.1.call-start = ((), (), s32[]{:S(2)}) async-start(), calls=%async_computation.9 | async-start | bytes 1572864 | tf_op jit(solution)/shard_map/all_gather | solution.py:121
  1139.8 16.0 %collective-permute-start.20 = (bf16[127,2048]{0,1:T(8,128)(2,1)S(1)}, bf16[127,2048]{0,1:T(8,128)(2,1)S(1)}, u32[]{:S(2)}, u32[]{:S(2)}) collective-permute-start(bf16[127,2048]{0,1:T(8,128)(2,1)S(1)} %bitcast.400), channel_id=1, source_target_pairs={{2,0},{4,2},{6,4},{8,6},{10,8},{12,10},{14,12},{16,14},{18,16},{20... | collective-permute-start | bytes 1560584 | tf_op jit(solution)/shard_map/ppermute | solution.py:11
  1183.0 15.2 collective-permute-start.21
  1234.8 308.3 %all-reduce.27.cloned.1.call-start = ((), (), s32[]{:S(2)}) async-start(), calls=%async_computation.10 | async-start | bytes 196608 | tf_op jit(solution)/shard_map/psum | solution.py:214
  1256.1 149.1 %collective-permute-start.23 = (bf16[127,2048]{0,1:T(8,128)(2,1)}, bf16[127,2048]{0,1:T(8,128)(2,1)}, u32[]{:S(2)}, u32[]{:S(2)}) collective-permute-start(bf16[127,2048]{0,1:T(8,128)(2,1)} %bitcast.354), channel_id=1, source_target_pairs={{2,0},{4,2},{6,4},{8,6},{10,8},{12,10},{14,12},{16,14},{18,16},{20... | collective-permute-start | bytes 1560584 | tf_op jit(solution)/shard_map/ppermute | solution.py:11
  (42 other events, 285.6 us)
Sparse Core Ops, SparseCore 0:
  28.8 17.0 all-gather.8
  426.4 52.9 all-gather.10
  548.2 59.8 all-gather.12
  676.8 60.5 all-gather.14
  806.3 61.3 all-gather.16
  936.6 60.4 all-gather.18
  1107.4 16.5 all-gather.20
  1234.9 15.4 all-gather.22
  1434.6 108.4 all-reduce.26
